TPU v7x, 512 devices: a whole 4x8x8 slice. The times are simulated.
512 devices in a mesh: fsdp: 64 (over y, x, core), cent: 8 (over z).
Axes of the slice: x: 4, y: 8, z: 8, core: 2. Of those that a mesh axis runs over, the one named last changes fastest.
Arguments:
- attention: bfloat16 [8192, 4096], P('fsdp', 'cent'), may hold values from -6 to 6
- w_out: bfloat16 [4096, 4096], P('cent', 'fsdp'), may hold values from -0.09375 to 0.09375
- hidden: bfloat16 [8192, 4096], P(('fsdp', 'cent')), may hold values from -6 to 6
- norm_gain: bfloat16 [4096], replicated, may hold values from 0.099609375 to 1.8984375
- centroids: bfloat16 [512, 4096], P('cent'), may hold values from -3 to 3
- token_codes: int32 [8192], P(('fsdp', 'cent')), may hold values from 0 to 63, as said below
- tile_lists: int32 [64, 8], P('fsdp'), may hold values from 0 to 63, as said below
Outputs:
- centroid_sums: float32 [512, 4096], P('cent', 'fsdp')
- residual_gram: float32 [4096, 4096], P('fsdp', 'cent')
Inputs may be any that keep to these rules, and one draw needn't show every extreme that they name: `token_codes`: token t belongs to block t // 128; its code k names centroid k % 8 of the tile at slot k // 8 of that block's list; every slot of a block's list is used. `tile_lists`: each row holds 8 distinct tile ids in ascending order; tile j holds centroids j * 8 to j * 8 + 7, and centroid g belongs to owner shard g // 64; in every row at most 2 listed tiles share an owner, and exactly 2 do for some owner.
All inputs are finite; a program needn't handle non-finite values.
Results may differ from a plain program's by a relative error of at most 0.0085.
Values may be sent and summed in bfloat16 or wider, within the bound.
A program may use at most 64 MiB of HBM per device.

v0:
```python
import jax
import jax.numpy as jnp
from jax import lax
from jax.sharding import PartitionSpec as P

TILE = 8
LT = 8


def shards(attention, w_out, hidden, norm_gain, centroids, token_codes, tile_lists):
    tok_dev = hidden.shape[0]
    feat_dim = hidden.shape[1]
    n_fsdp = lax.axis_size("fsdp")
    n_cent = lax.axis_size("cent")
    cap_slots = max(2, 2 * LT // n_cent)
    partial_out = jnp.dot(
        attention,
        lax.all_gather(w_out, "fsdp", axis=1, tiled=True),
        preferred_element_type=jnp.float32,
    )
    head_sum = lax.psum_scatter(
        partial_out.astype(jnp.bfloat16), "cent", scatter_dimension=0, tiled=True
    ).astype(jnp.float32)
    mixed_rows = hidden.astype(jnp.float32) + head_sum
    normed = (
        mixed_rows
        * lax.rsqrt(jnp.mean(mixed_rows * mixed_rows, axis=1, keepdims=True) + 1e-05)
        * norm_gain.astype(jnp.float32)
    )
    cent_dev = centroids.shape[0]
    own_tiles = cent_dev // TILE
    owner_idx = lax.axis_index("cent")
    listed = tile_lists[0]
    local_tile = listed - owner_idx * own_tiles
    owned_here = (local_tile >= 0) & (local_tile < own_tiles)
    safe_tile = jnp.clip(local_tile, 0, own_tiles - 1)
    tiles_here = centroids.reshape(own_tiles, TILE, feat_dim)
    slot_of = token_codes // TILE
    offset = token_codes % TILE
    rank_mine = jnp.cumsum(owned_here.astype(jnp.int32)) - 1
    chosen = owned_here[None, :] & (
        rank_mine[None, :] == jnp.arange(cap_slots, dtype=jnp.int32)[:, None]
    )
    send_tile = jnp.sum(jnp.where(chosen, safe_tile[None, :], 0), axis=1)
    filled = jnp.any(chosen, axis=1)
    outgoing = jnp.where(
        filled[:, None, None],
        jnp.take(tiles_here, send_tile, axis=0),
        jnp.zeros((cap_slots, TILE, feat_dim), jnp.bfloat16),
    )
    arrived = lax.all_gather(outgoing, "cent", axis=0, tiled=True)
    owner_of = listed // own_tiles
    list_pos = jnp.arange(LT, dtype=jnp.int32)
    earlier = (owner_of[None, :] == owner_of[:, None]) & (list_pos[None, :] < list_pos[:, None])
    rank_all = jnp.sum(earlier.astype(jnp.int32), axis=1)
    where_tile = owner_of * cap_slots + rank_all
    tile_rows = arrived.reshape(-1, feat_dim)
    centers = jnp.take(tile_rows, where_tile[slot_of] * TILE + offset, axis=0)
    residual = (normed - centers.astype(jnp.float32)).astype(jnp.bfloat16)
    onehot = (token_codes[None, :] == jnp.arange(LT * TILE, dtype=jnp.int32)[:, None]).astype(
        jnp.bfloat16
    )
    slot_part = jnp.dot(onehot, residual, preferred_element_type=jnp.float32)
    slot_sum = lax.psum(slot_part.astype(jnp.bfloat16), "cent").astype(jnp.float32)
    target = (local_tile[:, None] * TILE + jnp.arange(TILE, dtype=jnp.int32)[None, :]).reshape(-1)
    valid_rows = jnp.repeat(owned_here, TILE)
    placer = (
        (jnp.arange(cent_dev, dtype=jnp.int32)[:, None] == target[None, :]) & valid_rows[None, :]
    ).astype(jnp.float32)
    dense_part = jnp.dot(
        placer, slot_sum, precision=lax.Precision.HIGHEST, preferred_element_type=jnp.float32
    )
    centroid_sums = lax.psum_scatter(dense_part, "fsdp", scatter_dimension=1, tiled=True)
    rows_dev = feat_dim // n_fsdp
    row_start = lax.axis_index("fsdp") * rows_dev
    shard_rows = lax.all_gather(residual, "fsdp", axis=0, tiled=True)
    left_cols = lax.dynamic_slice_in_dim(shard_rows, row_start, rows_dev, 1)
    gram_part = lax.dot_general(
        left_cols, shard_rows, (((0,), (0,)), ((), ())), preferred_element_type=jnp.float32
    )
    gram_sum = lax.psum_scatter(gram_part, "cent", scatter_dimension=1, tiled=True)
    tokens_all = tok_dev * n_fsdp * n_cent
    return (centroid_sums, gram_sum / tokens_all)


def solution(mesh):
    in_specs = (
        P("fsdp", "cent"),
        P("cent", "fsdp"),
        P(("fsdp", "cent"), None),
        P(),
        P("cent", None),
        P(("fsdp", "cent")),
        P("fsdp", None),
    )
    out_specs = (P("cent", "fsdp"), P("fsdp", "cent"))
    return jax.shard_map(shards, mesh=mesh, in_specs=in_specs, out_specs=out_specs, check_vma=False)
```

profile of v0, /device:TPU:2, one launch (start us, length us, event | category | flops | bytes accessed | tf_op | source)
XLA Modules:
  0.0 561.0 jit_solution(6380447563696765636)
XLA Ops:
  7.2 0.0 copy-start
  7.2 0.0 copy-start.4
  7.2 0.0 copy-start.3
  7.2 0.0 all-gather.4.cloned.1.call-start
  7.3 0.7 all-gather.4.cloned.1.call-update
  7.9 0.0 all-gather.6.cloned.1.call-start
  8.0 0.7 convert_bitcast_fusion
  8.7 0.2 reduce-window.8
  8.9 0.7 fusion.11
  9.5 0.1 select_reduce_fusion
  9.7 0.0 copy-done
  9.7 0.6 gather_fusion.1
  10.2 0.1 fusion.8
  10.4 0.7 select_select_fusion
  11.1 0.0 all-gather.6.cloned.1.call-update
  11.1 0.0 reduce-scatter.6.cloned.1.call-start
  11.2 88.0 %all-gather.4.cloned.1.call-done = bf16[512,4096]{0,1:T(8,128)(2,1)} async-done(((bf16[512,64]{0,1:T(8,128)(2,1)}), bf16[512,4096]{0,1:T(8,128)(2,1)}) %all-gather.4.cloned.1.call-update) | async-done | bytes 4194320 | tf_op jit(solution)/shard_map/all_gather | solution.py:18
  99.2 4.8 convolution_convert_fusion
  104.0 0.0 reduce-scatter.6.cloned.1.call-update
  104.0 0.0 all-reduce.2.cloned.1.call-start
  104.1 0.2 convert_reduce_fusion
  104.3 0.7 gather_fusion
  105.0 37.3 %all-gather.6.cloned.1.call-done = bf16[16,8,4096]{2,1,0:T(8,128)(2,1)} async-done(((bf16[2,8,4096]{2,1,0:T(8,128)(2,1)}), bf16[16,8,4096]{2,1,0:T(8,128)(2,1)}) %all-gather.6.cloned.1.call-update) | async-done | bytes 1048592 | tf_op jit(solution)/shard_map/all_gather | solution.py:51
  142.4 2.1 gather_fusion.2
  144.5 41.3 %reduce-scatter.6.cloned.1.call-done = bf16[16,4096]{1,0:T(8,128)(2,1)} async-done(((bf16[128,4096]{1,0:T(8,128)(2,1)}), bf16[16,4096]{1,0:T(8,128)(2,1)}) %reduce-scatter.6.cloned.1.call-update) | async-done | bytes 131088 | tf_op jit(solution)/shard_map/reduce_scatter | solution.py:21
  185.8 1.1 multiply_reduce_fusion
  186.9 1.0 subtract_convert_fusion
  187.9 0.0 copy-start.1
  187.9 1.1 convolution_convert_fusion.1
  189.1 0.0 all-reduce.2.cloned.1.call-update
  189.1 0.0 all-gather.8.cloned.1.call-start
  189.1 0.5 all-gather.8.cloned.1.call-update
  189.7 0.0 reduce-scatter.10.cloned.1.call-start
  189.7 0.1 iota_add_fusion
  189.8 0.1 add.94
  189.9 0.1 broadcast_in_dim.69
  190.0 0.1 and.75
  190.1 77.2 %all-reduce.2.cloned.1.call-done = bf16[64,4096]{1,0:T(8,128)(2,1)} async-done(((bf16[64,4096]{1,0:T(8,128)(2,1)}), bf16[64,4096]{1,0:T(8,128)(2,1)}) %all-reduce.2.cloned.1.call-update) | async-done | bytes 524304 | tf_op jit(solution)/shard_map/psum | solution.py:64
  267.3 2.9 convolution_bitcast_fusion
  270.2 0.0 reduce-scatter.10.cloned.1.call-update
  270.2 0.0 reduce-scatter.8.cloned.1.call-start
  270.3 85.8 %all-gather.8.cloned.1.call-done = bf16[1024,4096]{1,0:T(8,128)(2,1)} async-done(((bf16[16,4096]{1,0:T(8,128)(2,1)}), bf16[1024,4096]{1,0:T(8,128)(2,1)}) %all-gather.8.cloned.1.call-update) | async-done | bytes 8388624 | tf_op jit(solution)/shard_map/all_gather | solution.py:76
  356.1 6.1 %fusion = f32[64,4096]{1,0:T(8,128)} fusion(bf16[1024,4096]{1,0:T(8,128)(2,1)} %all-gather.8.cloned.1.call-done, s32[]{:T(128)S(6)} %select_n.78), kind=kOutput, calls=%fused_computation.6 | convolution fusion | flops 536870912 | bytes 9699332 | tf_op jit(solution)/shard_map/dot_general | solution.py:78
  362.3 0.0 reduce-scatter.8.cloned.1.call-update
  362.3 145.4 %reduce-scatter.10.cloned.1.call-done = f32[64,64]{1,0:T(8,128)} async-done(((f32[4096,64]{1,0:T(8,128)}), f32[64,64]{1,0:T(8,128)}) %reduce-scatter.10.cloned.1.call-update) | async-done | bytes 16400
  507.7 1.5 copy.10
  509.1 43.5 %reduce-scatter.8.cloned.1.call-done = f32[64,512]{1,0:T(8,128)} async-done(((f32[64,4096]{1,0:T(8,128)}), f32[64,512]{1,0:T(8,128)}) %reduce-scatter.8.cloned.1.call-update) | async-done | bytes 131088 | tf_op jit(solution)/shard_map/reduce_scatter | solution.py:81
  552.6 1.6 broadcast_multiply_fusion
  (20 shorter events, 0.1 us)
Async XLA Ops:
  7.2 2.5 copy-start
  7.2 96.9 %copy-start.4 = (s32[1,8]{1,0:T(1,128)S(1)}, s32[1,8]{1,0:T(1,128)}, u32[]{:S(2)}) copy-start(s32[1,8]{1,0:T(1,128)} %param.13) | copy-start | bytes 100
  7.2 96.9 %copy-start.3 = (bf16[4096]{0:T(1024)(128)(2,1)S(1)}, bf16[4096]{0:T(1024)(128)(2,1)}, u32[]{:S(2)}) copy-start(bf16[4096]{0:T(1024)(128)(2,1)} %param.10) | copy-start | bytes 24580
  7.2 96.9 %copy-start.5 = (s32[16]{0:T(128)S(1)}, s32[16]{0:T(128)}, u32[]{:S(2)}) copy-start(s32[16]{0:T(128)} %param.12) | copy-start | bytes 196
  7.2 92.0 %all-gather.4.cloned.1.call-start = ((), (), s32[]{:S(2)}) async-start(), calls=%async_computation.3 | async-start | bytes 4259840 | tf_op jit(solution)/shard_map/all_gather | solution.py:18
  7.9 134.4 %all-gather.6.cloned.1.call-start = ((), (), s32[]{:S(2)}) async-start(), calls=%async_computation.5 | async-start | bytes 1179648 | tf_op jit(solution)/shard_map/all_gather | solution.py:51
  11.1 174.7 %copy-start.2 = (bf16[16,4096]{1,0:T(8,128)(2,1)S(1)}, bf16[16,4096]{1,0:T(8,128)(2,1)}, u32[]{:S(2)}) copy-start(bf16[16,4096]{1,0:T(8,128)(2,1)} %param.9) | copy-start | bytes 393220
  11.1 174.7 %reduce-scatter.6.cloned.1.call-start = ((), (), s32[]{:S(2)}) async-start(), calls=%async_computation.4 | async-start | bytes 1179648 | tf_op jit(solution)/shard_map/reduce_scatter | solution.py:21
  104.0 163.3 %all-reduce.2.cloned.1.call-start = ((), (), s32[]{:S(2)}) async-start(), calls=%async_computation.6 | async-start | bytes 1048576 | tf_op jit(solution)/shard_map/psum | solution.py:64
  187.9 1.2 copy-start.1
  189.1 167.0 %all-gather.8.cloned.1.call-start = ((), (), s32[]{:S(2)}) async-start(), calls=%async_computation.7 | async-start | bytes 8519680 | tf_op jit(solution)/shard_map/all_gather | solution.py:76
  189.7 318.0 %reduce-scatter.10.cloned.1.call-start = ((), (), s32[]{:S(2)}) async-start(), calls=%async_computation.9 | async-start | bytes 2129920
  270.2 282.3 %reduce-scatter.8.cloned.1.call-start = ((), (), s32[]{:S(2)}) async-start(), calls=%async_computation.8 | async-start | bytes 1179648 | tf_op jit(solution)/shard_map/reduce_scatter | solution.py:81
Sparse Core Ops, SparseCore 0:
  11.4 87.8 all-gather.3
  101.9 40.4 all-gather.5
  145.2 40.5 reduce-scatter.5
  189.2 78.0 all-reduce.1
  271.1 84.9 all-gather.7
  360.6 147.0 reduce-scatter.9
  510.5 42.0 reduce-scatter.7
where the time goes:
time: 561 us
  waiting for transfers between devices  520 us (93%)
  matrix products  15 us (3%)
  between operations  14.3 us (3%)
  other arithmetic  6.51 us (1%)
    unnamed x8, waiting for transfers between devices  147 us
    all_gather x1, waiting for transfers between devices, shards(): lax.all_gather(w_out, 'fsdp', axis=1, tiled=True)  88 us
    all_gather x1, waiting for transfers between devices, shards(): shard_rows = lax.all_gather(residual, 'fsdp', axis=0, tiled=True)  85.8 us
    psum x1, waiting for transfers between devices, shards(): lax.psum(slot_part.astype(jnp.bfloat16), 'cent').astype(jnp.float32)  77.2 us
    reduce_scatter x1, waiting for transfers between devices, shards(): lax.psum_scatter(gram_part, 'cent', scatter_dimension=1, tiled=True)  43.5 us
    reduce_scatter x1, waiting for transfers between devices, shards(): lax.psum_scatter(partial_out.astype(jnp.bfloat16), 'cent', scatter_dimens...  41.3 us
    all_gather x1, waiting for transfers between devices, shards(): arrived = lax.all_gather(outgoing, 'cent', axis=0, tiled=True)  37.3 us
  transfers between devices with their start and end apart: 7, of which 7 were waited for; matrix products, arithmetic and copies ran while one was open for 4% of the time, Pallas kernels for 0%

commit v1 on v0

--- a/solution.py
+++ b/solution.py
@@ -73,7 +73,9 @@
     centroid_sums = lax.psum_scatter(dense_part, "fsdp", scatter_dimension=1, tiled=True)
     rows_dev = feat_dim // n_fsdp
     row_start = lax.axis_index("fsdp") * rows_dev
-    shard_rows = lax.all_gather(residual, "fsdp", axis=0, tiled=True)
+    shard_rows = jnp.concatenate(
+        lax.all_to_all(jnp.stack([residual] * lax.axis_size("fsdp")), "fsdp", 0, 0), axis=0
+    )
     left_cols = lax.dynamic_slice_in_dim(shard_rows, row_start, rows_dev, 1)
     gram_part = lax.dot_general(
         left_cols, shard_rows, (((0,), (0,)), ((), ())), preferred_element_type=jnp.float32

time: 561 us -> 494 us (0.88)
  the two profiles are of different devices: /device:TPU:2 before, /device:TPU:4 now
where the time goes in v1:
time: 494 us
  waiting for transfers between devices  438 us (89%)
  matrix products  15 us (3%)
  between operations  14.3 us (3%)
  starting transfers between devices  10.7 us (2%)
  local copies, waits for them, and re-layouts  9.32 us (2%)
  other arithmetic  6.51 us (1%)
    all_to_all x1, waiting for transfers between devices, shards(): lax.all_to_all(jnp.stack([residual] * lax.axis_size('fsdp')), 'fsdp', 0, 0)  104 us
    all_gather x1, waiting for transfers between devices, shards(): lax.all_gather(w_out, 'fsdp', axis=1, tiled=True)  87.8 us
    psum x1, waiting for transfers between devices, shards(): lax.psum(slot_part.astype(jnp.bfloat16), 'cent').astype(jnp.float32)  79.6 us
    unnamed x7, waiting for transfers between devices  44.9 us
    reduce_scatter x1, waiting for transfers between devices, shards(): lax.psum_scatter(gram_part, 'cent', scatter_dimension=1, tiled=True)  43.3 us
    reduce_scatter x1, waiting for transfers between devices, shards(): lax.psum_scatter(partial_out.astype(jnp.bfloat16), 'cent', scatter_dimens...  41.3 us
    all_gather x1, waiting for transfers between devices, shards(): arrived = lax.all_gather(outgoing, 'cent', axis=0, tiled=True)  37.6 us
    all_to_all x1, starting transfers between devices, shards(): lax.all_to_all(jnp.stack([residual] * lax.axis_size('fsdp')), 'fsdp', 0, 0)  10.5 us
  transfers between devices with their start and end apart: 7, of which 7 were waited for; matrix products, arithmetic and copies ran while one was open for 5% of the time, Pallas kernels for 0%

profile of v1, /device:TPU:4, one launch (start us, length us, event | category | flops | bytes accessed | tf_op | source)
XLA Modules:
  0.0 493.9 jit_solution(17795808136419230780)
XLA Ops:
  7.2 0.0 copy-start
  7.2 0.0 copy-start.3
  7.2 0.0 copy-start.2
  7.2 0.0 all-gather.3.cloned.1.call-start
  7.3 0.7 all-gather.3.cloned.1.call-update
  7.9 0.0 all-gather.5.cloned.1.call-start
  8.0 0.7 convert_bitcast_fusion
  8.7 0.2 reduce-window.8
  8.9 0.7 fusion.11
  9.5 0.1 select_reduce_fusion
  9.7 0.6 gather_fusion.1
  10.2 0.1 fusion.8
  10.4 0.7 select_select_fusion
  11.1 0.0 all-gather.5.cloned.1.call-update
  11.1 0.0 reduce-scatter.6.cloned.1.call-start
  11.2 87.8 %all-gather.3.cloned.1.call-done = bf16[512,4096]{0,1:T(8,128)(2,1)} async-done(((bf16[512,64]{0,1:T(8,128)(2,1)}), bf16[512,4096]{0,1:T(8,128)(2,1)}) %all-gather.3.cloned.1.call-update) | async-done | bytes 4194320 | tf_op jit(solution)/shard_map/all_gather | solution.py:18
  99.0 4.7 convolution_convert_fusion
  103.7 0.0 reduce-scatter.6.cloned.1.call-update
  103.7 0.0 copy-done.2
  103.8 0.0 copy-done.4
  103.8 0.2 convert_reduce_fusion
  104.0 0.7 gather_fusion
  104.7 37.6 %all-gather.5.cloned.1.call-done = bf16[16,8,4096]{2,1,0:T(8,128)(2,1)} async-done(((bf16[2,8,4096]{2,1,0:T(8,128)(2,1)}), bf16[16,8,4096]{2,1,0:T(8,128)(2,1)}) %all-gather.5.cloned.1.call-update) | async-done | bytes 1048592 | tf_op jit(solution)/shard_map/all_gather | solution.py:51
  142.4 2.1 gather_fusion.2
  144.5 41.3 %reduce-scatter.6.cloned.1.call-done = bf16[16,4096]{1,0:T(8,128)(2,1)} async-done(((bf16[128,4096]{1,0:T(8,128)(2,1)}), bf16[16,4096]{1,0:T(8,128)(2,1)}) %reduce-scatter.6.cloned.1.call-update) | async-done | bytes 131088 | tf_op jit(solution)/shard_map/reduce_scatter | solution.py:21
  185.8 1.1 multiply_reduce_fusion
  186.9 1.0 subtract_convert_fusion
  187.9 4.3 stack.2
  192.2 10.5 %all-to-all-start = ((bf16[64,16,4096]{2,1,0:T(8,128)(2,1)}), bf16[64,16,4096]{2,1,0:T(8,128)(2,1)}, u32[]{:S(2)}, u32[]{:S(2)}) async-start(bf16[64,16,4096]{2,1,0:T(8,128)(2,1)} %stack.2), calls=%async_computation.1 | async-start | bytes 16777216 | tf_op jit(solution)/shard_map/all_to_all | solution.py:77
  202.6 0.0 all-reduce.2.cloned.1.call-start
  202.7 1.1 convolution_convert_fusion.1
  203.8 0.0 all-reduce.2.cloned.1.call-update
  203.8 0.0 reduce-scatter.10.cloned.1.call-start
  203.8 0.1 broadcast_in_dim.69
  203.9 0.1 and.75
  204.0 0.1 iota_add_fusion
  204.1 0.1 add.94
  204.2 79.6 %all-reduce.2.cloned.1.call-done = bf16[64,4096]{1,0:T(8,128)(2,1)} async-done(((bf16[64,4096]{1,0:T(8,128)(2,1)}), bf16[64,4096]{1,0:T(8,128)(2,1)}) %all-reduce.2.cloned.1.call-update) | async-done | bytes 524304 | tf_op jit(solution)/shard_map/psum | solution.py:64
  283.7 2.9 convolution_bitcast_fusion
  286.6 0.0 reduce-scatter.10.cloned.1.call-update
  286.7 0.0 reduce-scatter.8.cloned.1.call-start
  286.7 103.6 %all-to-all-done = bf16[64,16,4096]{2,1,0:T(8,128)(2,1)} async-done(((bf16[64,16,4096]{2,1,0:T(8,128)(2,1)}), bf16[64,16,4096]{2,1,0:T(8,128)(2,1)}, u32[]{:S(2)}, u32[]{:S(2)}) %all-to-all-start) | async-done | bytes 8388640 | tf_op jit(solution)/shard_map/all_to_all | solution.py:77
  390.3 6.3 %fusion = f32[64,4096]{1,0:T(8,128)} fusion(bf16[1024,4096]{1,0:T(8,128)(2,1)} %bitcast.10, s32[]{:T(128)S(6)} %select_n.78), kind=kOutput, calls=%fused_computation.6 | convolution fusion | flops 536870912 | bytes 9699332 | tf_op jit(solution)/shard_map/dot_general | solution.py:80
  396.6 0.0 reduce-scatter.8.cloned.1.call-update
  396.6 44.1 %reduce-scatter.10.cloned.1.call-done = f32[64,64]{1,0:T(8,128)} async-done(((f32[4096,64]{1,0:T(8,128)}), f32[64,64]{1,0:T(8,128)}) %reduce-scatter.10.cloned.1.call-update) | async-done | bytes 16400
  440.7 1.5 copy.10
  442.1 43.3 %reduce-scatter.8.cloned.1.call-done = f32[64,512]{1,0:T(8,128)} async-done(((f32[64,4096]{1,0:T(8,128)}), f32[64,512]{1,0:T(8,128)}) %reduce-scatter.8.cloned.1.call-update) | async-done | bytes 131088 | tf_op jit(solution)/shard_map/reduce_scatter | solution.py:83
  485.5 1.6 broadcast_multiply_fusion
  (18 shorter events, 0.1 us)
Async XLA Ops:
  7.2 2.5 copy-start
  7.2 96.6 %copy-start.3 = (s32[1,8]{1,0:T(1,128)S(1)}, s32[1,8]{1,0:T(1,128)}, u32[]{:S(2)}) copy-start(s32[1,8]{1,0:T(1,128)} %param.13) | copy-start | bytes 100
  7.2 96.6 %copy-start.2 = (bf16[4096]{0:T(1024)(128)(2,1)S(1)}, bf16[4096]{0:T(1024)(128)(2,1)}, u32[]{:S(2)}) copy-start(bf16[4096]{0:T(1024)(128)(2,1)} %param.10) | copy-start | bytes 24580
  7.2 96.6 %copy-start.4 = (s32[16]{0:T(128)S(1)}, s32[16]{0:T(128)}, u32[]{:S(2)}) copy-start(s32[16]{0:T(128)} %param.12) | copy-start | bytes 196
  7.2 91.8 %all-gather.3.cloned.1.call-start = ((), (), s32[]{:S(2)}) async-start(), calls=%async_computation.4 | async-start | bytes 4259840 | tf_op jit(solution)/shard_map/all_gather | solution.py:18
  7.9 134.4 %all-gather.5.cloned.1.call-start = ((), (), s32[]{:S(2)}) async-start(), calls=%async_computation.6 | async-start | bytes 1179648 | tf_op jit(solution)/shard_map/all_gather | solution.py:51
  11.1 174.7 %copy-start.1 = (bf16[16,4096]{1,0:T(8,128)(2,1)S(1)}, bf16[16,4096]{1,0:T(8,128)(2,1)}, u32[]{:S(2)}) copy-start(bf16[16,4096]{1,0:T(8,128)(2,1)} %param.9) | copy-start | bytes 393220
  11.1 174.7 %reduce-scatter.6.cloned.1.call-start = ((), (), s32[]{:S(2)}) async-start(), calls=%async_computation.5 | async-start | bytes 1179648 | tf_op jit(solution)/shard_map/reduce_scatter | solution.py:21
  192.2 198.1 %all-to-all-start = ((bf16[64,16,4096]{2,1,0:T(8,128)(2,1)}), bf16[64,16,4096]{2,1,0:T(8,128)(2,1)}, u32[]{:S(2)}, u32[]{:S(2)}) async-start(bf16[64,16,4096]{2,1,0:T(8,128)(2,1)} %stack.2), calls=%async_computation.1 | async-start | bytes 16777216 | tf_op jit(solution)/shard_map/all_to_all | solution.py:77
  202.6 81.1 %all-reduce.2.cloned.1.call-start = ((), (), s32[]{:S(2)}) async-start(), calls=%async_computation.7 | async-start | bytes 1048576 | tf_op jit(solution)/shard_map/psum | solution.py:64
  203.8 236.9 %reduce-scatter.10.cloned.1.call-start = ((), (), s32[]{:S(2)}) async-start(), calls=%async_computation.9 | async-start | bytes 2129920
  286.7 198.8 %reduce-scatter.8.cloned.1.call-start = ((), (), s32[]{:S(2)}) async-start(), calls=%async_computation.8 | async-start | bytes 1179648 | tf_op jit(solution)/shard_map/reduce_scatter | solution.py:83
Sparse Core Ops, SparseCore 0:
  11.4 87.5 all-gather.2
  101.6 40.6 all-gather.4
  145.2 40.5 reduce-scatter.5
  205.5 78.2 all-reduce.1
  288.2 152.4 reduce-scatter.9
  443.4 42.0 reduce-scatter.7
